TPU v7x, 32 devices: a whole 2x2x4 slice. The times are simulated.
32 devices in a mesh: station: 4 (over z), group: 4 (over x, core), bias: 2 (over y).
Axes of the slice: x: 2, y: 2, z: 4, core: 2. Of those that a mesh axis runs over, the one named last changes fastest.
Arguments:
- normal_mat: float32 [128, 2304], P(('station', 'group')), may hold values from -16 to 18, as said below
- coupling: float32 [128, 2, 8, 48, 128], P(('station', 'group'), 'bias'), may hold values from -0.13258252 to 0.13258252
- lengths: int32 [128], P(('station', 'group')), may hold values from 12 to 48
- visible: int32 [128, 2, 8], P(('station', 'group'), 'bias'), may hold values from 0 to 16, as said below
- bias_prior: float32 [2, 16, 128], P('bias', 'station'), may hold values from 0.1 to 1
- unimod: int32 [128, 2304], P(('station', 'group')), may hold values from -1 to 2, as said below
Outputs:
- bias_cov: float32 [2, 16, 128, 128], P('bias', 'station')
- amb_cov: float32 [128, 2304], P(('station', 'group'))
Inputs may be any that keep to these rules, and one draw needn't show every extreme that they name: `normal_mat`: each station's matrix, read as 48 x 48 row by row, is symmetric with all eigenvalues 1 or more. Each list visible[s, h] holds distinct block numbers below 16 in its first slots and the value 16 in its unused slots; every list has at least one block; in every draw the stations of some devices use all 8 slots. `unimod`: each station's matrix, read as 48 x 48 row by row, is a unit lower triangular times a unit upper triangular integer matrix; each row of the lower factor and each column of the upper factor holds at most one entry off the diagonal, -1 or 1; so every leading square block has determinant 1.
All inputs are finite; a program needn't handle non-finite values.
Results may differ from a plain program's by a relative error of at most 0.0003.
Values sent between devices are 32-bit elements; how exact they have to be, the bound alone decides.
No kernel may reach another device: no remote copies, remote signals or barrier semaphores. Data moves between devices by JAX's collectives and lax.ppermute only.
A program may use at most 64 MiB of HBM per device.

v0:
```python
import jax
import jax.numpy as jnp
from jax import lax
from jax.sharding import PartitionSpec as P

NHALF = 16
precise = lax.Precision.HIGHEST


def spd_inverse(matrix):
    matrix_order = matrix.shape[-1]
    factor = jnp.linalg.cholesky(matrix)
    identity = jnp.broadcast_to(jnp.eye(matrix_order, dtype=matrix.dtype), matrix.shape)
    lower_inv = lax.linalg.triangular_solve(factor, identity, left_side=True, lower=True)
    return jnp.einsum("...ka,...kb->...ab", lower_inv, lower_inv, precision=precise)


def prepare(normal_mat, coupling, lengths):
    stations = coupling.shape[0]
    block_len = coupling.shape[3]
    positions = jnp.arange(block_len, dtype=jnp.int32)
    row_valid = (positions[None, :] < lengths[:, None]).astype(jnp.float32)
    keep_mask = row_valid[:, :, None] * row_valid[:, None, :]
    stacked = normal_mat.reshape(stations, block_len, block_len)
    effective = keep_mask * stacked + (1.0 - keep_mask) * jnp.eye(block_len, dtype=jnp.float32)
    inverse = spd_inverse(effective)
    weighted = coupling * row_valid[:, None, None, :, None]
    solved = jnp.einsum("sab,shjbc->shjac", inverse, weighted, precision=precise)
    return (keep_mask, inverse, weighted, solved)


def finish_cov(keep_mask, inverse, bias_part, unimod):
    stations = keep_mask.shape[0]
    block_len = keep_mask.shape[1]
    covariance = keep_mask * (inverse + bias_part)
    integer_map = unimod.reshape(stations, block_len, block_len).astype(jnp.float32)
    mapped = jnp.einsum("sab,sbc,sdc->sad", integer_map, covariance, integer_map, precision=precise)
    return (keep_mask * mapped).reshape(stations, block_len * block_len)


def local(normal_mat, coupling, lengths, visible, bias_prior, unimod):
    keep_mask, inverse, weighted, solved = prepare(normal_mat, coupling, lengths)
    reduced = jnp.einsum("shjac,shjad->shjcd", weighted, weighted - solved, precision=precise)
    block_width = coupling.shape[4]
    identity = jnp.eye(block_width, dtype=jnp.float32)
    columns = jnp.arange(NHALF, dtype=jnp.int32)
    selector = (visible[..., None] == columns).astype(jnp.float32)
    block_table = jnp.einsum("shjx,shjcd->hxcd", selector, reduced, precision=precise)
    local_sum = lax.psum_scatter(block_table, "station", scatter_dimension=1, tiled=True)
    block_sum = lax.psum(local_sum, "group")
    bias_cov = spd_inverse(block_sum + bias_prior[..., :, None] * identity)
    segment = lax.all_gather(bias_cov, "station", axis=1, tiled=True)
    piece_len = segment.shape[1]
    local_pick = (visible[..., None] == jnp.arange(piece_len, dtype=jnp.int32)).astype(jnp.float32)
    chosen = jnp.einsum("shjx,hxcd->shjcd", local_pick, segment, precision=precise)
    lifted = jnp.einsum("shjac,shjcd->shjad", solved, chosen, precision=precise)
    bias_part = jnp.einsum("shjad,shjbd->sab", lifted, solved, precision=precise)
    combined = lax.psum(bias_part.reshape(bias_part.shape[0], -1), "bias")
    amb_cov = finish_cov(keep_mask, inverse, combined.reshape(bias_part.shape), unimod)
    return (bias_cov, amb_cov)


def solution(mesh):
    return jax.shard_map(
        local,
        mesh=mesh,
        in_specs=(
            P(("station", "group"), None),
            P(("station", "group"), "bias", None, None, None),
            P(("station", "group")),
            P(("station", "group"), "bias", None),
            P("bias", "station", None),
            P(("station", "group"), None),
        ),
        out_specs=(P("bias", "station", None, None), P(("station", "group"), None)),
        check_vma=False,
    )
```

profile of v0, /device:TPU:0, one launch (start us, length us, event | category | flops | bytes accessed | tf_op | source)
XLA Modules:
  0.0 314.8 jit_solution(5613608994066356341)
XLA Ops:
  7.2 0.0 reduce-scatter.2.cloned.1.call-start
  7.3 0.7 fusion.43
  8.0 0.1 copy.56
  8.1 1.0 reshape.177
  9.1 0.1 copy.55
  9.2 0.0 copy-start
  9.2 0.1 fusion.24
  9.3 0.1 copy.57
  9.4 0.1 fusion.30
  9.6 35.2 %custom-call.14 = f32[8,48,48]{2,1,0:T(8,128)S(1)} custom-call(f32[8,48,48]{2,1,0:T(8,128)S(1)} %fusion.30), custom_call_target="Cholesky" | custom-call | tf_op jit(solution)/shard_map/jit(cholesky)/cholesky | solution.py:12
  44.8 0.1 compare_reduce_fusion
  44.9 0.1 select_bitcast_fusion.1
  45.0 29.5 %custom-call.15 = f32[8,1,48,48]{2,3,1,0:T(8,128)S(1)} custom-call(f32[8,1,48,48]{3,2,1,0:T(8,128)S(1)} %select_bitcast_fusion.1), custom_call_target="InvertDiagBlocksLowerTriangular" | custom-call | tf_op jit(solution)/shard_map/triangular_solve | solution.py:14
  74.6 0.5 fusion.28
  75.1 0.5 fusion.44
  75.6 0.0 copy-done
  75.6 1.7 fusion.10
  77.3 0.0 copy-start.2
  77.3 6.9 %fusion.7 = f32[8,8,128,128]{3,2,1,0:T(8,128)S(1)} fusion(f32[8,8,128,48]{2,3,1,0:T(8,128)S(1)} %fusion.10, f32[8,1,8,48,128]{4,3,2,1,0:T(8,128)S(1)} %copy-done, f32[8,48]{1,0:T(8,128)S(1)} %fusion.43), kind=kOutput, calls=%fused_computation.9 | convolution fusion | flops 605159424 | bytes 7341568 | tf_op jit(solution)/shard_map/shjac,shjad->shjcd/dot_general | solution.py:43
  84.2 0.0 copy-done.2
  84.2 4.1 %fusion.12 = f32[16,128,128]{2,0,1:T(8,128)S(1)} fusion(f32[8,8,128,128]{3,2,1,0:T(8,128)S(1)} %fusion.7, s32[8,8]{1,0:T(8,128)S(1)} %bitcast.86), kind=kOutput, calls=%fused_computation.14 | convolution fusion | flops 201327616 | bytes 5243136 | tf_op jit(solution)/shard_map/shjx,shjcd->hxcd/dot_general | solution.py:48
  88.3 0.0 copy-start.3
  88.3 1.4 copy.62
  89.8 0.0 reduce-scatter.2.cloned.1.call-update
  89.8 0.0 all-reduce.3.cloned.1.call-start
  89.9 30.1 %reduce-scatter.2.cloned.1.call-done = f32[1,4,128,128]{2,3,1,0:T(8,128)} async-done(((f32[1,16,128,128]{2,3,1,0:T(8,128)}), f32[1,4,128,128]{2,3,1,0:T(8,128)}) %reduce-scatter.2.cloned.1.call-update) | async-done | bytes 262160 | tf_op jit(solution)/shard_map/reduce_scatter | solution.py:49
  120.0 0.0 all-reduce.3.cloned.1.call-update
  120.0 0.0 all-gather.3.cloned.1.call-start
  120.1 0.1 copy.63
  120.2 32.9 %all-reduce.3.cloned.1.call-done = f32[1,4,128,128]{2,3,1,0:T(8,128)} async-done(((f32[1,4,128,128]{2,3,1,0:T(8,128)}), f32[1,4,128,128]{2,3,1,0:T(8,128)}) %all-reduce.3.cloned.1.call-update) | async-done | bytes 262160 | tf_op jit(solution)/shard_map/psum | solution.py:50
  153.1 0.0 copy-done.3
  153.1 1.0 multiply_add_fusion
  154.1 0.1 copy.64
  154.2 1.0 fusion.23
  155.3 46.9 %custom-call.16 = f32[1,4,128,128]{3,2,1,0:T(8,128)S(1)} custom-call(f32[1,4,128,128]{3,2,1,0:T(8,128)S(1)} %fusion.23), custom_call_target="Cholesky" | custom-call | tf_op jit(solution)/shard_map/jit(cholesky)/cholesky | solution.py:12
  202.2 0.1 compare_reduce_fusion.1
  202.3 0.1 select_bitcast_fusion
  202.4 39.3 %custom-call.17 = f32[1,4,1,128,128]{3,4,2,1,0:T(8,128)S(1)} custom-call(f32[1,4,1,128,128]{4,3,2,1,0:T(8,128)S(1)} %select_bitcast_fusion), custom_call_target="InvertDiagBlocksLowerTriangular" | custom-call | tf_op jit(solution)/shard_map/triangular_solve | solution.py:14
  241.8 0.6 fusion.21
  242.3 1.3 fusion.45
  243.7 0.0 all-gather.3.cloned.1.call-update
  243.7 0.3 all-reduce.5.cloned.1.call-start
  243.9 27.9 %all-gather.3.cloned.1.call-done = f32[16,128,128]{2,1,0:T(8,128)} async-done(((f32[4,128,128]{2,1,0:T(8,128)}), f32[16,128,128]{2,1,0:T(8,128)}) %all-gather.3.cloned.1.call-update) | async-done | bytes 1048592 | tf_op jit(solution)/shard_map/all_gather | solution.py:52
  271.8 3.3 %convolution_bitcast_fusion = f32[8,8,128,128]{3,1,0,2:T(8,128)S(1)} fusion(f32[16,128,128,1]{2,1,0,3:T(8,128)} %bitcast.85, s32[8,8]{1,0:T(8,128)S(1)} %bitcast.87), kind=kOutput, calls=%fused_computation.4 | convolution fusion | flops 201327616 | bytes 5243136 | tf_op jit(solution)/shard_map/shjx,hxcd->shjcd/dot_general | solution.py:55
  275.1 6.0 %fusion = f32[8,8,48,128]{3,2,1,0:T(8,128)S(1)} fusion(f32[8,8,128,48]{2,3,1,0:T(8,128)S(1)} %fusion.10, f32[8,8,128,128]{3,1,0,2:T(8,128)S(1)} %convolution_bitcast_fusion), kind=kOutput, calls=%fused_computation | convolution fusion | flops 603979776 | bytes 7340032 | tf_op jit(solution)/shard_map/shjac,shjcd->shjad/dot_general | solution.py:56
  281.1 0.0 copy-start.1
  281.1 2.4 fusion.15
  283.5 0.0 all-reduce.5.cloned.1.call-update
  283.5 0.1 copy.70
  283.6 0.0 copy-done.1
  283.7 0.1 convert_element_type.47
  283.8 21.7 %all-reduce.5.cloned.1.call-done = f32[8,48,48]{1,2,0:T(8,128)} async-done(((f32[8,48,48]{1,2,0:T(8,128)}), f32[8,48,48]{1,2,0:T(8,128)}) %all-reduce.5.cloned.1.call-update) | async-done | bytes 73744 | tf_op jit(solution)/shard_map/psum | solution.py:58
  305.5 1.4 fusion.26
  306.9 0.4 convolution_multiply_fusion
  307.4 0.1 copy.73
  307.5 0.8 reshape.185
  (9 shorter events, 0.2 us)
Async XLA Ops:
  7.2 112.8 %reduce-scatter.2.cloned.1.call-start = ((), (), s32[]{:S(2)}) async-start(), calls=%async_computation.1 | async-start | bytes 1310720 | tf_op jit(solution)/shard_map/reduce_scatter | solution.py:49
  9.2 66.4 %copy-start = (f32[8,1,8,48,128]{4,3,2,1,0:T(8,128)S(1)}, f32[8,1,8,48,128]{4,3,2,1,0:T(8,128)}, u32[]{:S(2)}) copy-start(f32[8,1,8,48,128]{4,3,2,1,0:T(8,128)} %param.7) | copy-start | bytes 4718596
  77.3 6.9 %copy-start.2 = (s32[8,1,8]{2,1,0:T(1,128)S(1)}, s32[8,1,8]{2,1,0:T(1,128)}, u32[]{:S(2)}) copy-start(s32[8,1,8]{2,1,0:T(1,128)} %param.9) | copy-start | bytes 772
  88.3 64.8 %copy-start.3 = (f32[1,4,128]{2,1,0:T(4,128)S(1)}, f32[1,4,128]{2,1,0:T(4,128)}, u32[]{:S(2)}) copy-start(f32[1,4,128]{2,1,0:T(4,128)} %param.10) | copy-start | bytes 6148
  89.8 63.3 %all-reduce.3.cloned.1.call-start = ((), (), s32[]{:S(2)}) async-start(), calls=%async_computation.2 | async-start | bytes 524288 | tf_op jit(solution)/shard_map/psum | solution.py:50
  120.0 151.8 %all-gather.3.cloned.1.call-start = ((), (), s32[]{:S(2)}) async-start(), calls=%async_computation.4 | async-start | bytes 1310720 | tf_op jit(solution)/shard_map/all_gather | solution.py:52
  243.7 61.8 %all-reduce.5.cloned.1.call-start = ((), (), s32[]{:S(2)}) async-start(), calls=%async_computation.3 | async-start | bytes 393216 | tf_op jit(solution)/shard_map/psum | solution.py:58
  281.1 2.5 copy-start.1
Sparse Core Ops, SparseCore 0:
  89.9 29.9 reduce-scatter.1
  122.3 30.7 all-reduce.2
  243.8 27.9 all-gather.2
  283.6 21.7 all-reduce.4
where the time goes:
time: 315 us
  other arithmetic  154 us (49%)
  waiting for transfers between devices  113 us (36%)
  matrix products  29.1 us (9%)
  between operations  14.1 us (4%)
  local copies, waits for them, and re-layouts  4.08 us (1%)
    another operation x8, other arithmetic, spd_inverse(): factor = jnp.linalg.cholesky(matrix)  82.4 us
    another operation x6, other arithmetic, spd_inverse(): lax.linalg.triangular_solve(factor, identity, left_side=True, lower=True)  69.1 us
    psum x1, waiting for transfers between devices, local(): block_sum = lax.psum(local_sum, 'group')  32.9 us
    reduce_scatter x1, waiting for transfers between devices, local(): lax.psum_scatter(block_table, 'station', scatter_dimension=1, tiled=True)  30.1 us
    all_gather x1, waiting for transfers between devices, local(): segment = lax.all_gather(bias_cov, 'station', axis=1, tiled=True)  27.9 us
    psum x1, waiting for transfers between devices, local(): combined = lax.psum(bias_part.reshape(bias_part.shape[0], -1), 'bias')  21.7 us
    dot_general x1, matrix products, local(): jnp.einsum('shjac,shjad->shjcd', weighted, weighted - solved, precision=p...  6.89 us
  transfers between devices with their start and end apart: 4, of which 4 were waited for; matrix products, arithmetic and copies ran while one was open for 0% of the time, Pallas kernels for 0%

commit v1 on v0

--- a/solution.py
+++ b/solution.py
@@ -47,7 +47,11 @@
     selector = (visible[..., None] == columns).astype(jnp.float32)
     block_table = jnp.einsum("shjx,shjcd->hxcd", selector, reduced, precision=precise)
     local_sum = lax.psum_scatter(block_table, "station", scatter_dimension=1, tiled=True)
-    block_sum = lax.psum(local_sum, "group")
+    block_sum = local_sum
+    for hop in (1, 2):
+        block_sum = block_sum + lax.ppermute(
+            block_sum, "group", [(dev, dev ^ hop) for dev in range(4)]
+        )
     bias_cov = spd_inverse(block_sum + bias_prior[..., :, None] * identity)
     segment = lax.all_gather(bias_cov, "station", axis=1, tiled=True)
     piece_len = segment.shape[1]

time: 315 us -> 290 us (0.921)
  waiting for transfers between devices: 113 us -> 86.7 us
    psum x1 -> x0, waiting for transfers between devices: 32.9 us -> none  [local(): block_sum = lax.psum(local_sum, 'group')]
    ppermute x0 -> x2, waiting for transfers between devices: none -> 8.46 us  [local(): lax.ppermute(block_sum, 'group', [(dev, dev ^ hop) for dev in range(4)])]
  transfers between devices with their start and end apart: 4 -> 5, of which waited for: 4 -> 5; matrix products, arithmetic and copies ran while one was open for 0% -> 0% of each run, Pallas kernels for 0% -> 0%
where the time goes in v1:
time: 290 us; the launch traced here: 289 us
  other arithmetic  154 us (53%)
  waiting for transfers between devices  86.7 us (30%)
  matrix products  29.1 us (10%)
  between operations  14 us (5%)
  local copies, waits for them, and re-layouts  4.08 us (1%)
    another operation x8, other arithmetic, spd_inverse(): factor = jnp.linalg.cholesky(matrix)  82.4 us
    another operation x6, other arithmetic, spd_inverse(): lax.linalg.triangular_solve(factor, identity, left_side=True, lower=True)  69.1 us
    reduce_scatter x1, waiting for transfers between devices, local(): lax.psum_scatter(block_table, 'station', scatter_dimension=1, tiled=True)  30.1 us
    all_gather x1, waiting for transfers between devices, local(): segment = lax.all_gather(bias_cov, 'station', axis=1, tiled=True)  26.4 us
    psum x1, waiting for transfers between devices, local(): combined = lax.psum(bias_part.reshape(bias_part.shape[0], -1), 'bias')  21.7 us
    ppermute x2, waiting for transfers between devices, local(): lax.ppermute(block_sum, 'group', [(dev, dev ^ hop) for dev in range(4)])  8.46 us
    dot_general x1, matrix products, local(): jnp.einsum('shjac,shjad->shjcd', weighted, weighted - solved, precision=p...  6.89 us
    dot_general x1, matrix products, local(): lifted = jnp.einsum('shjac,shjcd->shjad', solved, chosen, precision=precise)  5.97 us
  transfers between devices with their start and end apart: 5, of which 5 were waited for; matrix products, arithmetic and copies ran while one was open for 0% of the time, Pallas kernels for 0%

profile of v1, /device:TPU:0, one launch (start us, length us, event | category | flops | bytes accessed | tf_op | source)
XLA Modules:
  0.0 289.4 jit_solution(2880634829708052729)
XLA Ops:
  7.2 0.0 reduce-scatter.2.cloned.1.call-start
  7.3 0.7 fusion.43
  8.0 0.1 copy.56
  8.1 1.0 reshape.177
  9.1 0.1 copy.55
  9.2 0.0 copy-start
  9.2 0.1 fusion.24
  9.3 0.1 copy.57
  9.4 0.1 fusion.30
  9.6 35.2 %custom-call.14 = f32[8,48,48]{2,1,0:T(8,128)S(1)} custom-call(f32[8,48,48]{2,1,0:T(8,128)S(1)} %fusion.30), custom_call_target="Cholesky" | custom-call | tf_op jit(solution)/shard_map/jit(cholesky)/cholesky | solution.py:12
  44.8 0.1 compare_reduce_fusion
  44.9 0.1 select_bitcast_fusion.1
  45.0 29.5 %custom-call.15 = f32[8,1,48,48]{2,3,1,0:T(8,128)S(1)} custom-call(f32[8,1,48,48]{3,2,1,0:T(8,128)S(1)} %select_bitcast_fusion.1), custom_call_target="InvertDiagBlocksLowerTriangular" | custom-call | tf_op jit(solution)/shard_map/triangular_solve | solution.py:14
  74.6 0.5 fusion.28
  75.1 0.5 fusion.44
  75.6 0.0 copy-done
  75.6 1.7 fusion.10
  77.3 0.0 copy-start.2
  77.3 6.9 %fusion.7 = f32[8,8,128,128]{3,2,1,0:T(8,128)S(1)} fusion(f32[8,8,128,48]{2,3,1,0:T(8,128)S(1)} %fusion.10, f32[8,1,8,48,128]{4,3,2,1,0:T(8,128)S(1)} %copy-done, f32[8,48]{1,0:T(8,128)S(1)} %fusion.43), kind=kOutput, calls=%fused_computation.9 | convolution fusion | flops 605159424 | bytes 7341568 | tf_op jit(solution)/shard_map/shjac,shjad->shjcd/dot_general | solution.py:43
  84.2 0.0 copy-done.2
  84.2 4.1 %fusion.12 = f32[16,128,128]{2,0,1:T(8,128)S(1)} fusion(f32[8,8,128,128]{3,2,1,0:T(8,128)S(1)} %fusion.7, s32[8,8]{1,0:T(8,128)S(1)} %bitcast.86), kind=kOutput, calls=%fused_computation.14 | convolution fusion | flops 201327616 | bytes 5243136 | tf_op jit(solution)/shard_map/shjx,shjcd->hxcd/dot_general | solution.py:48
  88.3 0.0 copy-start.3
  88.3 1.4 copy.62
  89.8 0.0 reduce-scatter.2.cloned.1.call-update
  89.8 0.0 all-gather.3.cloned.1.call-start
  89.9 30.1 %reduce-scatter.2.cloned.1.call-done = f32[1,4,128,128]{2,3,1,0:T(8,128)} async-done(((f32[1,16,128,128]{2,3,1,0:T(8,128)}), f32[1,4,128,128]{2,3,1,0:T(8,128)}) %reduce-scatter.2.cloned.1.call-update) | async-done | bytes 262160 | tf_op jit(solution)/shard_map/reduce_scatter | solution.py:49
  120.0 0.0 collective-permute-start
  120.0 1.7 collective-permute-done
  121.7 1.0 add.43
  122.7 1.5 collective-permute-start.1
  124.3 0.1 copy.63
  124.4 6.7 %collective-permute-done.1 = f32[1,4,128,128]{2,3,1,0:T(8,128)S(1)} collective-permute-done((f32[1,4,128,128]{2,3,1,0:T(8,128)S(1)}, f32[1,4,128,128]{2,3,1,0:T(8,128)S(1)}, u32[]{:S(2)}, u32[]{:S(2)}) %collective-permute-start.1) | collective-permute-done | bytes 262176 | tf_op jit(solution)/shard_map/ppermute | solution.py:52
  131.1 0.0 copy-done.3
  131.2 0.1 copy.64
  131.3 46.9 %custom-call.16 = f32[1,4,128,128]{3,2,1,0:T(8,128)S(1)} custom-call(f32[1,4,128,128]{3,2,1,0:T(8,128)S(1)} %fusion.23), custom_call_target="Cholesky" | custom-call | tf_op jit(solution)/shard_map/jit(cholesky)/cholesky | solution.py:12
  178.3 0.1 compare_reduce_fusion.1
  178.4 0.1 select_bitcast_fusion
  178.5 39.3 %custom-call.17 = f32[1,4,1,128,128]{3,4,2,1,0:T(8,128)S(1)} custom-call(f32[1,4,1,128,128]{4,3,2,1,0:T(8,128)S(1)} %select_bitcast_fusion), custom_call_target="InvertDiagBlocksLowerTriangular" | custom-call | tf_op jit(solution)/shard_map/triangular_solve | solution.py:14
  217.8 0.6 fusion.21
  218.4 1.3 fusion.45
  219.7 0.0 all-gather.3.cloned.1.call-update
  219.7 0.3 all-reduce.2.cloned.1.call-start
  220.0 26.4 %all-gather.3.cloned.1.call-done = f32[16,128,128]{2,1,0:T(8,128)} async-done(((f32[4,128,128]{2,1,0:T(8,128)}), f32[16,128,128]{2,1,0:T(8,128)}) %all-gather.3.cloned.1.call-update) | async-done | bytes 1048592 | tf_op jit(solution)/shard_map/all_gather | solution.py:56
  246.4 3.3 %convolution_bitcast_fusion = f32[8,8,128,128]{3,1,0,2:T(8,128)S(1)} fusion(f32[16,128,128,1]{2,1,0,3:T(8,128)} %bitcast.85, s32[8,8]{1,0:T(8,128)S(1)} %bitcast.87), kind=kOutput, calls=%fused_computation.4 | convolution fusion | flops 201327616 | bytes 5243136 | tf_op jit(solution)/shard_map/shjx,hxcd->shjcd/dot_general | solution.py:59
  249.7 6.0 %fusion = f32[8,8,48,128]{3,2,1,0:T(8,128)S(1)} fusion(f32[8,8,128,48]{2,3,1,0:T(8,128)S(1)} %fusion.10, f32[8,8,128,128]{3,1,0,2:T(8,128)S(1)} %convolution_bitcast_fusion), kind=kOutput, calls=%fused_computation | convolution fusion | flops 603979776 | bytes 7340032 | tf_op jit(solution)/shard_map/shjac,shjcd->shjad/dot_general | solution.py:60
  255.7 0.0 copy-start.1
  255.7 2.4 fusion.15
  258.1 0.0 all-reduce.2.cloned.1.call-update
  258.1 0.1 copy.70
  258.2 0.0 copy-done.1
  258.3 0.1 convert_element_type.47
  258.4 21.7 %all-reduce.2.cloned.1.call-done = f32[8,48,48]{1,2,0:T(8,128)} async-done(((f32[8,48,48]{1,2,0:T(8,128)}), f32[8,48,48]{1,2,0:T(8,128)}) %all-reduce.2.cloned.1.call-update) | async-done | bytes 73744 | tf_op jit(solution)/shard_map/psum | solution.py:62
  280.1 1.4 fusion.26
  281.5 0.4 convolution_multiply_fusion
  281.9 0.1 copy.73
  282.1 0.8 reshape.185
  (11 shorter events, 0.2 us)
Async XLA Ops:
  7.2 112.8 %reduce-scatter.2.cloned.1.call-start = ((), (), s32[]{:S(2)}) async-start(), calls=%async_computation.1 | async-start | bytes 1310720 | tf_op jit(solution)/shard_map/reduce_scatter | solution.py:49
  9.2 66.4 %copy-start = (f32[8,1,8,48,128]{4,3,2,1,0:T(8,128)S(1)}, f32[8,1,8,48,128]{4,3,2,1,0:T(8,128)}, u32[]{:S(2)}) copy-start(f32[8,1,8,48,128]{4,3,2,1,0:T(8,128)} %param.7) | copy-start | bytes 4718596
  77.3 6.9 %copy-start.2 = (s32[8,1,8]{2,1,0:T(1,128)S(1)}, s32[8,1,8]{2,1,0:T(1,128)}, u32[]{:S(2)}) copy-start(s32[8,1,8]{2,1,0:T(1,128)} %param.9) | copy-start | bytes 772
  88.3 42.8 %copy-start.3 = (f32[1,4,128]{2,1,0:T(4,128)S(1)}, f32[1,4,128]{2,1,0:T(4,128)}, u32[]{:S(2)}) copy-start(f32[1,4,128]{2,1,0:T(4,128)} %param.10) | copy-start | bytes 6148
  89.8 156.6 %all-gather.3.cloned.1.call-start = ((), (), s32[]{:S(2)}) async-start(), calls=%async_computation.3 | async-start | bytes 1310720 | tf_op jit(solution)/shard_map/all_gather | solution.py:56
  120.0 1.7 collective-permute-start
  122.7 8.4 %collective-permute-start.1 = (f32[1,4,128,128]{2,3,1,0:T(8,128)S(1)}, f32[1,4,128,128]{2,3,1,0:T(8,128)S(1)}, u32[]{:S(2)}, u32[]{:S(2)}) collective-permute-start(f32[1,4,128,128]{2,3,1,0:T(8,128)S(1)} %add.43), channel_id=1, source_target_pairs={{0,4},{2,6},{4,0},{6,2},{1,5},{3,7},{5,1},{7,3},{8,12},{10,14},{12... | collective-permute-start | bytes 786440 | tf_op jit(solution)/shard_map/ppermute | solution.py:52
  219.7 60.3 %all-reduce.2.cloned.1.call-start = ((), (), s32[]{:S(2)}) async-start(), calls=%async_computation.2 | async-start | bytes 393216 | tf_op jit(solution)/shard_map/psum | solution.py:62
  255.7 2.5 copy-start.1
Sparse Core Ops, SparseCore 0:
  89.9 29.9 reduce-scatter.1
  219.9 26.4 all-gather.2
  258.2 21.7 all-reduce.1
